TPU v7x, 1024 devices: a whole 4x4x32 slice. The times are simulated.
1024 devices in a mesh: enc: 32 (over z), llm: 4 (over x), tp: 8 (over y, core).
Axes of the slice: x: 4, y: 4, z: 32, core: 2. Of those that a mesh axis runs over, the one named last changes fastest.
Arguments:
- visual: bfloat16 [32, 4, 32, 4, 8192], P('enc', 'llm'), may hold values from -6 to 6
- counts: int32 [32, 4, 32], P('enc', 'llm'), may hold values from 0 to 4, as said below
- merger_bias: float32 [8192], replicated, may hold values from -3 to 3
- norm_gain: float32 [8192], replicated, may hold values from 0.1 to 1.9
- kv_weight: bfloat16 [8192, 2048], P(None, 'tp'), may hold values from -0.0625 to 0.0625
- kv_cotangent: bfloat16 [32, 4, 32, 4, 2048], P('enc', 'llm', None, None, 'tp'), may hold values from -6 to 6
Outputs:
- key_values: bfloat16 [32, 4, 32, 4, 2048], P('enc', 'llm', None, None, 'tp')
- visual_grad: bfloat16 [32, 4, 32, 4, 8192], P('enc', 'llm', None, None, 'tp')
- bias_grad: float32 [8192], P('tp')
Inputs may be any that keep to these rules, and one draw needn't show every extreme that they name: Slots c < counts[s, g, b] of block (s, g, b) hold live merged patch blocks, the others hold unused data. For every group g some bucket b receives 4 live slots from every source s.
All inputs are finite; a program needn't handle non-finite values.
Results may differ from a plain program's by a relative error of at most 0.0049.
Values may be sent and summed in bfloat16 or wider, within the bound.
A program may use at most 64 MiB of HBM per device.

v0:
```python
import jax
import jax.numpy as jnp
from jax import lax
from jax.sharding import PartitionSpec as P


def per_device(visual, counts, merger_bias, norm_gain, kv_weight, kv_cotangent):
    enc_count = lax.axis_size("enc")
    tp_count = lax.axis_size("tp")
    capacity = visual.shape[3]
    features = visual.shape[4]
    own_width = features // tp_count
    own_start = lax.axis_index("tp") * own_width
    columns = kv_weight.shape[1]
    total_rows = enc_count * capacity
    arrived, got_counts = (
        lax.all_to_all(visual[0, 0], "enc", split_axis=0, concat_axis=0, tiled=True),
        lax.all_to_all(counts[0, 0], "enc", split_axis=0, concat_axis=0, tiled=True),
    )
    flat_rows = arrived.reshape(total_rows, features)
    validity = (
        lax.broadcasted_iota(jnp.int32, (enc_count, capacity), 1) < got_counts[:, None]
    ).reshape(total_rows, 1)
    inputs = flat_rows.astype(jnp.float32) + merger_bias
    inv_rms = lax.rsqrt(jnp.mean(inputs * inputs, axis=1, keepdims=True) + 1e-06)
    normed = (inputs * inv_rms * norm_gain).astype(jnp.bfloat16)
    projected = jnp.dot(normed, kv_weight, preferred_element_type=jnp.float32)
    key_out = jnp.where(validity, projected, jnp.zeros_like(projected)).astype(jnp.bfloat16)
    cot_rows = kv_cotangent[0, 0].reshape(total_rows, columns)
    masked = jnp.where(validity, cot_rows, jnp.zeros_like(cot_rows))
    part_dots = jnp.sum(masked.astype(jnp.float32) * projected, axis=1, keepdims=True)
    grad_part = lax.dot_general(
        masked, kv_weight, (((1,), (1,)), ((), ())), preferred_element_type=jnp.float32
    )
    dots_wide = jnp.broadcast_to(part_dots, (total_rows, tp_count))
    grad_normed, row_dot = (
        lax.psum_scatter(grad_part, "tp", scatter_dimension=1, tiled=True),
        lax.psum_scatter(dots_wide, "tp", scatter_dimension=1, tiled=True),
    )
    own_inputs = lax.dynamic_slice_in_dim(inputs, own_start, own_width, 1)
    own_gain = lax.dynamic_slice_in_dim(norm_gain, own_start, own_width, 0)
    grad_rows = (
        inv_rms * own_gain * grad_normed - own_inputs * (inv_rms * inv_rms) * row_dot / features
    )
    bias_part = jnp.sum(grad_rows, axis=0)
    bias_grad = lax.psum(bias_part, ("enc", "llm"))
    returned = lax.all_to_all(
        grad_rows.astype(jnp.bfloat16).reshape(enc_count, capacity, own_width),
        "enc",
        split_axis=0,
        concat_axis=0,
        tiled=True,
    )
    visual_grad = returned.reshape(1, 1, enc_count, capacity, own_width)
    key_values = key_out.reshape(1, 1, enc_count, capacity, columns)
    return (key_values, visual_grad, bias_grad)


def solution(mesh):
    return jax.shard_map(
        per_device,
        mesh=mesh,
        in_specs=(
            P("enc", "llm", None, None, None),
            P("enc", "llm", None),
            P(),
            P(),
            P(None, "tp"),
            P("enc", "llm", None, None, "tp"),
        ),
        out_specs=(P("enc", "llm", None, None, "tp"), P("enc", "llm", None, None, "tp"), P("tp")),
        check_vma=False,
    )
```

profile of v0, /device:TPU:2, one launch (start us, length us, event | category | flops | bytes accessed | tf_op | source)
XLA Modules:
  0.0 590.2 jit_solution(12595712203107001332)
XLA Ops:
  7.2 0.0 copy-start.3
  7.2 0.8 copy.10
  7.9 50.9 %all_to_all.19 = s32[32,1,1]{2,1,0:T(1,128)S(1)} all-to-all(s32[32,1,1]{2,1,0:T(1,128)S(1)} %copy.10), channel_id=1, replica_groups=mesh['enc'=32,'llm'=4,'tp'=8] {'enc'}, dimensions={0} | all-to-all | bytes 256 | tf_op jit(solution)/shard_map/all_to_all | solution.py:18
  58.9 4.0 all-to-all-start.1
  62.9 0.0 reduce-scatter.2.cloned.1.call-start
  63.0 0.0 copy-done.3
  63.0 0.7 reduce.1
  63.6 0.1 iota_compare_fusion
  63.7 0.1 lt.24
  63.8 5.6 fusion.3
  69.5 0.0 copy-start.2
  69.5 0.0 reduce-scatter.2.cloned.1.call-update
  69.5 1.3 dynamic-slice
  70.8 191.1 %all-to-all-done.1 = bf16[32,4,8192]{2,1,0:T(4,128)(2,1)S(1)} async-done(((bf16[32,4,8192]{2,1,0:T(4,128)(2,1)}), bf16[32,4,8192]{2,1,0:T(4,128)(2,1)S(1)}, u32[]{:S(2)}, u32[]{:S(2)}) %all-to-all-start.1) | async-done | bytes 2097184 | tf_op jit(solution)/shard_map/all_to_all | solution.py:17
  261.8 0.0 copy-done.2
  261.8 1.4 multiply_reduce_fusion
  263.3 0.1 rsqrt.15
  263.4 2.5 reshape.72
  265.9 0.0 copy-start.1
  265.9 0.0 copy-start.4
  265.9 2.7 broadcast_add_fusion
  268.6 0.7 copy-done.1
  269.4 0.0 copy-done.4
  269.4 0.0 copy-start
  269.4 0.0 dynamic-slice-start
  269.4 0.8 select_convert_fusion
  270.1 1.2 copy-done
  271.3 0.2 multiply_reduce_fusion.1
  271.5 12.4 %all-reduce = f32[128,8]{0,1:T(8,128)S(1)} all-reduce(f32[128,8]{0,1:T(8,128)S(1)} %broadcast_in_dim.34), channel_id=3, replica_groups=mesh['enc'=32,'llm'=4,'tp'=8] {'tp'}, use_global_device_ids=true, to_apply=%region_3.4.clone | all-reduce | flops 1024 | bytes 8192
  283.9 0.6 dynamic-slice_bitcast_fusion
  284.6 0.0 reduce-scatter.2.cloned.1.call-done
  284.6 0.0 dynamic-slice-done
  284.6 1.4 fusion.5
  286.1 0.8 reshape.70
  286.9 4.7 all-to-all-start.2
  291.6 0.7 reshape.69
  292.2 290.5 %psum.7 = f32[1024]{0:T(1024)} all-reduce(f32[1024]{0:T(1024)S(1)} %get-tuple-element.3), channel_id=1, replica_groups=mesh['enc'=32,'llm'=4,'tp'=8] {'enc','llm'}, use_global_device_ids=true, to_apply=%region_5.6 | all-reduce | flops 1024 | bytes 8192 | tf_op jit(solution)/shard_map/psum | solution.py:46
  582.7 0.0 all-to-all-done.2
  582.7 0.7 copy.12
  (4 shorter events, 0.0 us)
Async XLA Ops:
  7.2 55.8 %copy-start.3 = (bf16[1,1,32,4,256]{4,3,2,1,0:T(4,128)(2,1)S(1)}, bf16[1,1,32,4,256]{4,3,2,1,0:T(4,128)(2,1)}, u32[]{:S(2)}) copy-start(bf16[1,1,32,4,256]{4,3,2,1,0:T(4,128)(2,1)} %param.11) | copy-start | bytes 196612
  58.9 203.0 %all-to-all-start.1 = ((bf16[32,4,8192]{2,1,0:T(4,128)(2,1)}), bf16[32,4,8192]{2,1,0:T(4,128)(2,1)S(1)}, u32[]{:S(2)}, u32[]{:S(2)}) async-start(bf16[32,4,8192]{2,1,0:T(4,128)(2,1)} %bitcast.8), calls=%async_computation.1 | async-start | bytes 4194304 | tf_op jit(solution)/shard_map/all_to_all | solution.py:17
  62.9 221.7 %reduce-scatter.2.cloned.1.call-start = ((), (), s32[]{:S(2)}) async-start(), calls=%async_computation.4 | async-start | bytes 4718592 | tf_op jit(solution)/shard_map/reduce_scatter | solution.py:37
  69.5 192.4 %copy-start.2 = (f32[8192]{0:T(1024)S(1)}, f32[8192]{0:T(1024)}, u32[]{:S(2)}) copy-start(f32[8192]{0:T(1024)} %param.8) | copy-start | bytes 98308
  265.9 3.4 copy-start.1
  265.9 3.4 copy-start.4
  269.4 2.0 copy-start
  269.4 15.3 %dynamic-slice-start = ((f32[8192]{0:T(1024)}, s32[]{:T(128)}), f32[1024]{0:T(1024)S(1)}, s32[]{:S(2)}) async-start(f32[8192]{0:T(1024)} %param.9, s32[]{:T(128)} %select_n.13), calls=%async_computation.5 | async-start | bytes 8704 | tf_op jit(solution)/shard_map/dynamic_slice | solution.py:41
  286.9 295.8 %all-to-all-start.2 = ((bf16[32,4,1024]{2,1,0:T(4,128)(2,1)}), bf16[32,4,1024]{2,1,0:T(4,128)(2,1)S(1)}, u32[]{:S(2)}, u32[]{:S(2)}) async-start(bf16[32,4,1024]{2,1,0:T(4,128)(2,1)} %reshape.70), calls=%async_computation.3 | async-start | bytes 524288 | tf_op jit(solution)/shard_map/all_to_all | solution.py:47
Sparse Core Ops, SparseCore 0:
  69.6 56.9 reduce-scatter.1
where the time goes:
time: 591 us; the launch traced here: 590 us
  blocking collectives  354 us (60%)
  waiting for transfers between devices  191 us (32%)
  between operations  14.2 us (2%)
  local copies, waits for them, and re-layouts  9.52 us (2%)
  starting transfers between devices  8.77 us (1%)
  other arithmetic  6.5 us (1%)
  matrix products  6.36 us (1%)
    psum x1, blocking collectives, per_device(): bias_grad = lax.psum(bias_part, ('enc', 'llm'))  290 us
    all_to_all x1, waiting for transfers between devices, per_device(): lax.all_to_all(visual[0, 0], 'enc', split_axis=0, concat_axis=0, tiled=True)  191 us
    all_to_all x1, blocking collectives, per_device(): lax.all_to_all(counts[0, 0], 'enc', split_axis=0, concat_axis=0, tiled=True)  50.9 us
    unnamed x1, blocking collectives  12.4 us
  transfers between devices with their start and end apart: 3, of which 1 were waited for; matrix products, arithmetic and copies ran while one was open for 3% of the time, Pallas kernels for 0%

commit v1 on v0

v1 whole, which is shorter than its diff:
```python
import jax
import jax.numpy as jnp
from jax import lax
from jax.sharding import PartitionSpec as P


def per_device(visual, counts, merger_bias, norm_gain, kv_weight, kv_cotangent):
    buckets, capacity, features = visual.shape[2:]
    tp_count = lax.axis_size("tp")
    own_width = features // tp_count
    own_start = lax.axis_index("tp") * own_width
    columns = kv_weight.shape[1]
    rows = buckets * capacity
    cot_rows = lax.all_to_all(
        kv_cotangent[0, 0], "enc", split_axis=0, concat_axis=0, tiled=True
    ).reshape(rows, columns)
    live = (
        lax.broadcasted_iota(jnp.int32, (buckets, capacity), 1) < counts[0, 0][:, None]
    ).reshape(rows, 1)
    inputs = visual[0, 0].reshape(rows, features).astype(jnp.float32) + merger_bias
    inv_rms = lax.rsqrt(jnp.mean(inputs * inputs, axis=1, keepdims=True) + 1e-06)
    normed = (inputs * inv_rms * norm_gain).astype(jnp.bfloat16)
    projected = jnp.dot(normed, kv_weight, preferred_element_type=jnp.float32)
    key_out = jnp.where(live, projected, jnp.zeros_like(projected)).astype(jnp.bfloat16)
    key_values = lax.all_to_all(
        key_out.reshape(buckets, capacity, columns), "enc", split_axis=0, concat_axis=0, tiled=True
    )
    masked = jnp.where(live, cot_rows, jnp.zeros_like(cot_rows))
    part_dots = jnp.sum(masked.astype(jnp.float32) * projected, axis=1, keepdims=True)
    grad_part = lax.dot_general(
        masked, kv_weight, (((1,), (1,)), ((), ())), preferred_element_type=jnp.float32
    )
    grad_normed = lax.psum_scatter(
        grad_part.astype(jnp.bfloat16), "tp", scatter_dimension=1, tiled=True
    ).astype(jnp.float32)
    row_dot = lax.psum(part_dots, "tp")
    own_inputs = lax.dynamic_slice_in_dim(inputs, own_start, own_width, 1)
    own_gain = lax.dynamic_slice_in_dim(norm_gain, own_start, own_width, 0)
    grad_rows = (
        inv_rms * own_gain * grad_normed - own_inputs * (inv_rms * inv_rms) * row_dot / features
    )
    bias_grad = lax.psum(jnp.sum(grad_rows, axis=0), ("enc", "llm"))
    visual_grad = grad_rows.astype(jnp.bfloat16).reshape(1, 1, buckets, capacity, own_width)
    return (key_values[None, None], visual_grad, bias_grad)


def solution(mesh):
    return jax.shard_map(
        per_device,
        mesh=mesh,
        in_specs=(
            P("enc", "llm", None, None, None),
            P("enc", "llm", None),
            P(),
            P(),
            P(None, "tp"),
            P("enc", "llm", None, None, "tp"),
        ),
        out_specs=(P("enc", "llm", None, None, "tp"), P("enc", "llm", None, None, "tp"), P("tp")),
        check_vma=False,
    )
```

time: 591 us -> 404 us (0.68)
  waiting for transfers between devices: 191 us -> 49.4 us
  blocking collectives: 354 us -> 288 us
  starting transfers between devices: 8.77 us -> 32.6 us
    all_to_all x2, waiting for transfers between devices: 191 us -> 49.4 us  [the longest x1 24.9 us: per_device(): lax.all_to_all(kv_cotangent[0, 0], 'enc', split_axis=0, concat_axis=0, ti...]
    all_to_all x1 -> x0, blocking collectives: 50.9 us -> none  [per_device(): lax.all_to_all(counts[0, 0], 'enc', split_axis=0, concat_axis=0, tiled=True)]
    all_to_all x2, starting transfers between devices: 8.73 us -> 32.6 us  [the longest x1 28.7 us: per_device(): lax.all_to_all(kv_cotangent[0, 0], 'enc', split_axis=0, concat_axis=0, ti...]
    unnamed x1 -> x0, blocking collectives: 12.4 us -> none
    psum x1 -> x2, blocking collectives: 290 us -> 288 us  [the longest x1 276 us: per_device(): bias_grad = lax.psum(jnp.sum(grad_rows, axis=0), ('enc', 'llm'))]
  transfers between devices with their start and end apart: 3 -> 3, of which waited for: 1 -> 2; matrix products, arithmetic and copies ran while one was open for 3% -> 2% of each run, Pallas kernels for 0% -> 0%
where the time goes in v1:
time: 404 us; the launch traced here: 403 us
  blocking collectives  288 us (71%)
  waiting for transfers between devices  49.4 us (12%)
  starting transfers between devices  32.6 us (8%)
  between operations  14.1 us (3%)
  local copies, waits for them, and re-layouts  6.7 us (2%)
  other arithmetic  6.43 us (2%)
  matrix products  5.91 us (1%)
    psum x1, blocking collectives, per_device(): bias_grad = lax.psum(jnp.sum(grad_rows, axis=0), ('enc', 'llm'))  276 us
    all_to_all x1, starting transfers between devices, per_device(): lax.all_to_all(kv_cotangent[0, 0], 'enc', split_axis=0, concat_axis=0, ti...  28.7 us
    all_to_all x1, waiting for transfers between devices, per_device(): lax.all_to_all(kv_cotangent[0, 0], 'enc', split_axis=0, concat_axis=0, ti...  24.9 us
    all_to_all x1, waiting for transfers between devices, per_device(): lax.all_to_all(key_out.reshape(buckets, capacity, columns), 'enc', split_...  24.5 us
    psum x1, blocking collectives, per_device(): row_dot = lax.psum(part_dots, 'tp')  12.4 us
  transfers between devices with their start and end apart: 3, of which 2 were waited for; matrix products, arithmetic and copies ran while one was open for 2% of the time, Pallas kernels for 0%

profile of v1, /device:TPU:2, one launch (start us, length us, event | category | flops | bytes accessed | tf_op | source)
XLA Modules:
  0.0 403.4 jit_solution(3038741956155985688)
XLA Ops:
  7.2 28.7 %all-to-all-start.1 = ((bf16[32,4,256]{2,1,0:T(4,128)(2,1)}), bf16[32,4,256]{2,1,0:T(4,128)(2,1)S(1)}, u32[]{:S(2)}, u32[]{:S(2)}) async-start(bf16[32,4,256]{2,1,0:T(4,128)(2,1)} %bitcast.6), calls=%async_computation.1 | async-start | bytes 131072 | tf_op jit(solution)/shard_map/all_to_all | solution.py:14
  35.9 0.0 reduce-scatter.2.cloned.1.call-start
  36.0 0.7 iota_compare_fusion
  36.7 0.1 lt.24
  36.8 24.9 %all-to-all-done.1 = bf16[32,4,256]{2,1,0:T(4,128)(2,1)S(1)} async-done(((bf16[32,4,256]{2,1,0:T(4,128)(2,1)}), bf16[32,4,256]{2,1,0:T(4,128)(2,1)S(1)}, u32[]{:S(2)}, u32[]{:S(2)}) %all-to-all-start.1) | async-done | bytes 65568 | tf_op jit(solution)/shard_map/all_to_all | solution.py:14
  61.7 0.0 copy-start.2
  61.7 5.2 %convolution_convert_fusion = bf16[128,8192]{1,0:T(8,128)(2,1)} fusion(bf16[8192,256]{1,0:T(8,128)(2,1)} %param.10, bf16[128,256]{1,0:T(8,128)(2,1)S(1)} %reshape.64, pred[128]{0:T(512)(128)(4,1)S(1)} %lt.24), kind=kOutput, calls=%fused_computation | convolution fusion | flops 537952256 | bytes 6357120 | tf_op jit(solution)/shard_map/dot_general | solution.py:30
  66.9 0.0 copy-start.3
  66.9 0.0 reduce-scatter.2.cloned.1.call-update
  66.9 0.0 copy-done.2
  66.9 2.5 reshape.67
  69.4 0.0 copy-done.3
  69.4 1.4 multiply_reduce_fusion
  70.9 0.1 rsqrt.15
  71.0 0.0 copy-start.1
  71.0 0.0 copy-start.4
  71.0 2.7 broadcast_add_fusion
  73.7 0.7 copy-done.1
  74.4 0.0 copy-done.4
  74.4 0.0 copy-start
  74.4 0.8 select_convert_fusion
  75.2 1.2 copy-done
  76.4 0.6 reshape.63
  77.0 3.9 all-to-all-start
  80.9 24.5 %all-to-all-done = bf16[32,4,256]{2,1,0:T(4,128)(2,1)S(1)} async-done(((bf16[32,4,256]{2,1,0:T(4,128)(2,1)}), bf16[32,4,256]{2,1,0:T(4,128)(2,1)S(1)}, u32[]{:S(2)}, u32[]{:S(2)}) %all-to-all-start) | async-done | bytes 65568 | tf_op jit(solution)/shard_map/all_to_all | solution.py:25
  105.4 0.2 multiply_reduce_fusion.1
  105.6 12.4 %psum.14 = f32[128]{0:T(128)S(1)} all-reduce(f32[128]{0:T(128)S(1)} %multiply_reduce_fusion.1), channel_id=1, replica_groups=mesh['enc'=32,'llm'=4,'tp'=8] {'tp'}, use_global_device_ids=true, to_apply=%region_3.4 | all-reduce | flops 128 | bytes 1024 | tf_op jit(solution)/shard_map/psum | solution.py:36
  118.0 0.0 reduce-scatter.2.cloned.1.call-done
  118.0 1.3 fusion.4
  119.3 275.8 %psum.15 = f32[1024]{0:T(1024)} all-reduce(f32[1024]{0:T(1024)S(1)} %get-tuple-element.3), channel_id=1, replica_groups=mesh['enc'=32,'llm'=4,'tp'=8] {'enc','llm'}, use_global_device_ids=true, to_apply=%region_5.6 | all-reduce | flops 1024 | bytes 8192 | tf_op jit(solution)/shard_map/psum | solution.py:42
  395.1 0.8 reshape.65
  395.9 0.6 copy.10
  (4 shorter events, 0.0 us)
Async XLA Ops:
  7.2 54.5 %all-to-all-start.1 = ((bf16[32,4,256]{2,1,0:T(4,128)(2,1)}), bf16[32,4,256]{2,1,0:T(4,128)(2,1)S(1)}, u32[]{:S(2)}, u32[]{:S(2)}) async-start(bf16[32,4,256]{2,1,0:T(4,128)(2,1)} %bitcast.6), calls=%async_computation.1 | async-start | bytes 131072 | tf_op jit(solution)/shard_map/all_to_all | solution.py:14
  35.9 82.1 %reduce-scatter.2.cloned.1.call-start = ((), (), s32[]{:S(2)}) async-start(), calls=%async_computation.3 | async-start | bytes 2359296 | tf_op jit(solution)/shard_map/reduce_scatter | solution.py:33
  61.7 5.2 %copy-start.2 = (bf16[1,1,32,4,8192]{4,3,2,1,0:T(4,128)(2,1)S(1)}, bf16[1,1,32,4,8192]{4,3,2,1,0:T(4,128)(2,1)}, u32[]{:S(2)}) copy-start(bf16[1,1,32,4,8192]{4,3,2,1,0:T(4,128)(2,1)} %param.6) | copy-start | bytes 6291460
  66.9 2.5 copy-start.3
  71.0 3.5 copy-start.1
  71.0 3.4 copy-start.4
  74.4 1.9 copy-start
  77.0 28.4 %all-to-all-start = ((bf16[32,4,256]{2,1,0:T(4,128)(2,1)}), bf16[32,4,256]{2,1,0:T(4,128)(2,1)S(1)}, u32[]{:S(2)}, u32[]{:S(2)}) async-start(bf16[32,4,256]{2,1,0:T(4,128)(2,1)} %reshape.63), calls=%async_computation | async-start | bytes 131072 | tf_op jit(solution)/shard_map/all_to_all | solution.py:25
Sparse Core Ops, SparseCore 0:
  67.0 33.3 reduce-scatter.1

commit v2 on v1

v2 whole, which is shorter than its diff:
```python
import functools

import jax
import jax.numpy as jnp
from jax import lax
from jax.experimental import pallas as pl
from jax.experimental.pallas import tpu as pltpu
from jax.sharding import PartitionSpec as P

RING = 4
LANES = 128
UNIT = 256


def remote(src, dst, send, recv, **where):
    return pltpu.make_async_remote_copy(
        src_ref=src,
        dst_ref=dst,
        send_sem=send,
        recv_sem=recv,
        device_id=where,
        device_id_type=pl.DeviceIdType.MESH,
    )


def kernel(
    counts, bias, gain, vis_hbm, w_hbm, cot_hbm,
    kv_out, vg_out, bg_out,
    vis, w, cot_own, cot_in, xs, xn, inv, proj, kv_own, masked, coef,
    s1, r1, acc, s2, r2, s3, r3, vg,
    p_own, p_in, q_own, q_in, z_own, z_in, f_own, f_in,
    cot_s, cot_r, kv_s, kv_r, z_s, z_r, p_s, p_r, q_s, q_r, f_s, f_r,
    s1_s, s1_r, s2_s, s2_r, s3_s, s3_r, loc,
):
    n_enc, n_llm = lax.axis_size("enc"), lax.axis_size("llm")
    n_tp = lax.axis_size("tp")
    me, group, rank = lax.axis_index("enc"), lax.axis_index("llm"), lax.axis_index("tp")
    chip, core = rank // 2, rank % 2
    units = w.shape[0]
    per_rank = units // n_tp
    features = units * UNIT
    rows = n_enc * 4
    pairs = n_enc // 2

    barrier = pltpu.get_barrier_semaphore()

    def far(i):
        step = (i + 1) // 2
        return lax.rem(me + n_enc // 2 + step * (1 - 2 * lax.rem(i, 2)), n_enc)

    @pl.loop(0, n_enc - 1)
    def _(i):
        pl.semaphore_signal(barrier, 1, device_id={"enc": far(i)})

    for d in range(1, n_llm):
        pl.semaphore_signal(barrier, 1, device_id={"llm": lax.rem(group + d, n_llm)})
    for d in range(1, n_tp):
        pl.semaphore_signal(barrier, 1, device_id={"tp": lax.rem(rank + d, n_tp)})

    get_vis = pltpu.make_async_copy(vis_hbm.at[0, 0], vis, loc.at[0])
    get_w = pltpu.make_async_copy(w_hbm, w, loc.at[1])
    get_cot = pltpu.make_async_copy(cot_hbm.at[0, 0], cot_own, loc.at[2])
    get_vis.start()
    get_w.start()
    get_cot.start()

    get_vis.wait()

    @pl.loop(0, pairs // 2)
    def _(g):
        for h in range(2):
            i = g * 2 + h
            squares = jnp.zeros((8, UNIT), jnp.float32)
            for u in range(units):
                cols = slice(u * UNIT, (u + 1) * UNIT)
                add = bias[:, cols]
                xs[u, i, 0:4, :] = vis[2 * i, :, cols].astype(jnp.float32) + add
                xs[u, i, 4:8, :] = vis[2 * i + 1, :, cols].astype(jnp.float32) + add
                x = xs[u, i]
                squares = squares + x * x
            mean = jnp.sum(squares, axis=1, keepdims=True) * (1.0 / features)
            inv[i] = jnp.broadcast_to(lax.rsqrt(mean + 1e-06), (8, LANES))
        scale = inv[pl.ds(2 * g, 2)].reshape(16, LANES)[:, :1]
        for u in range(units):
            x = xs[u, pl.ds(2 * g, 2)].reshape(16, UNIT)
            xn[u, g] = (x * scale * gain[u]).astype(jnp.bfloat16)

    get_w.wait()
    proj[...] = jnp.zeros_like(proj)

    @pl.loop(0, units)
    def _(u):
        proj[...] += jnp.dot(
            xn[u].reshape(rows, UNIT), w[u], preferred_element_type=jnp.float32
        ).reshape(proj.shape)

    slot = lax.broadcasted_iota(jnp.int32, (4, UNIT), 0)

    @pl.loop(0, pairs)
    def _(i):
        for h in range(2):
            rows4 = proj[i, 4 * h : 4 * h + 4, :]
            kept = jnp.where(slot < counts[0, 0, 2 * i + h], rows4, 0.0)
            kv_own[2 * i + h] = kept.astype(jnp.bfloat16)

    get_cot.wait()
    pl.semaphore_wait(barrier, n_enc - 1 + n_llm - 1 + n_tp - 1)

    def cot_copy(other, at):
        return remote(
            cot_own.at[other], cot_in.at[at], cot_s.at[other], cot_r.at[at], enc=other
        )

    @pl.loop(0, n_enc - 1)
    def _(i):
        cot_copy(far(i), me).start()

    cot_in[me] = cot_own[me]

    @pl.loop(0, n_enc - 1)
    def _(i):
        other = lax.rem(me + 1 + i, n_enc)
        cot_copy(other, other).wait_recv()

    def kv_copy(other, at):
        return remote(
            kv_own.at[other], kv_out.at[0, 0, at], kv_s.at[other], kv_r.at[at], enc=other
        )

    @pl.loop(0, n_enc - 1)
    def _(i):
        kv_copy(far(i), me).start()

    kv_self = pltpu.make_async_copy(kv_own.at[me], kv_out.at[0, 0, me], loc.at[3])
    kv_self.start()

    @pl.loop(0, pairs)
    def _(i):
        for h in range(2):
            got = cot_in[2 * i + h].astype(jnp.float32)
            masked[i, 4 * h : 4 * h + 4, :] = jnp.where(slot < counts[0, 0, 2 * i + h], got, 0.0)
        dots = jnp.sum(masked[i] * proj[i], axis=1, keepdims=True)
        coef[i] = inv[i] * inv[i] * jnp.broadcast_to(dots, (8, LANES)) * (1.0 / features)

    def term(u):
        cot16 = masked[...].reshape(rows, UNIT).astype(jnp.bfloat16)
        grad = lax.dot_general(
            cot16, w[u], (((1,), (1,)), ((), ())), preferred_element_type=jnp.float32
        )
        a = inv[...].reshape(rows, LANES)[:, :1]
        b = coef[...].reshape(rows, LANES)[:, :1]
        return a * gain[u] * grad - xs[u].reshape(rows, UNIT) * b

    def column_sums(j, v, part):
        total = jnp.sum(part, axis=0, keepdims=True)
        for k in range(UNIT // LANES):
            p_own[j, pl.ds(v * (UNIT // LANES) + k, 1), :] = total[:, k * LANES : (k + 1) * LANES]

    def s1_copy(k):
        return remote(s1.at[k], r1.at[k], s1_s.at[k], s1_r.at[k], tp=rank + 1 - 2 * core)

    order = (2, 1, 3, 0)
    for k in order:
        j = lax.rem(chip + k, RING) * 2 + 1 - core
        for v in range(per_rank):
            part = term(j * per_rank + v)
            s1[k, v] = part.astype(jnp.bfloat16)
            column_sums(j, v, part)
        s1_copy(k).start()
    for k in order:
        j = lax.rem(chip + k, RING) * 2 + core
        for v in range(per_rank):
            part = term(j * per_rank + v)
            acc[k, v] = part
            column_sums(j, v, part)

    def p_copy(other, at):
        return remote(p_own.at[other], p_in.at[at], p_s.at[other], p_r.at[at], tp=other)

    for d in range(1, n_tp):
        p_copy(lax.rem(rank + d, n_tp), rank).start()
    p_in[rank] = p_own[rank]

    half = rows // 2

    def pair(k):
        s1_copy(k).wait_recv()
        for v in range(per_rank):
            acc[k, v] += r1[k, v].astype(jnp.float32)

    up = lax.rem(chip + 1, RING) * 2 + core
    down = lax.rem(chip + RING - 1, RING) * 2 + core

    def s2_copy(h):
        return remote(s2.at[h], r2.at[h], s2_s.at[h], s2_r.at[h], tp=(up, down)[h])

    def s3_copy(side, h):
        return remote(
            s3.at[side, h], r3.at[side, h], s3_s.at[side, h], s3_r.at[side, h], tp=(up, down)[side]
        )

    def fill(dst, k, h):
        for v in range(per_rank):
            dst[v] = acc[k, v, h * half : (h + 1) * half, :].astype(jnp.bfloat16)

    pair(2)
    for h in range(2):
        fill(s2.at[h], 2, h)
        s2_copy(h).start()
    for side, k in ((0, 1), (1, 3)):
        pair(k)
        fill(s3.at[side, 1 - side], k, 1 - side)
        s3_copy(side, 1 - side).start()

    for d in range(1, n_tp):
        other = lax.rem(rank + d, n_tp)
        p_copy(other, other).wait_recv()
    q = p_in[0]
    for t in range(1, n_tp):
        q = q + p_in[t]
    q_rows = 8 // n_llm
    for g in range(n_llm):
        q_own[g] = q[g * q_rows : (g + 1) * q_rows, :]

    def q_copy(other, at):
        return remote(q_own.at[other], q_in.at[at], q_s.at[other], q_r.at[at], llm=other)

    for d in range(1, n_llm):
        q_copy(lax.rem(group + d, n_llm), group).start()
    q_in[group] = q_own[group]

    pair(0)
    for side, k in ((0, 1), (1, 3)):
        s2_copy(side).wait_recv()
        for v in range(per_rank):
            acc[k, v, side * half : (side + 1) * half, :] += r2[side, v].astype(jnp.float32)
        fill(s3.at[side, side], k, side)
        s3_copy(side, side).start()

    for d in range(1, n_llm):
        other = lax.rem(group + d, n_llm)
        q_copy(other, other).wait_recv()
    q = q_in[0]
    for g in range(1, n_llm):
        q = q + q_in[g]
    z_own[...] = q

    def z_copy(other, at):
        return remote(z_own, z_in.at[at], z_s.at[other], z_r.at[at], enc=other)

    @pl.loop(0, n_enc - 1)
    def _(i):
        z_copy(far(i), me).start()

    z_in[me] = q

    for h in range(2):
        for side in range(2):
            s3_copy(side, h).wait_recv()
        for v in range(per_rank):
            total = acc[0, v, h * half : (h + 1) * half, :] + (
                r3[0, h, v].astype(jnp.float32) + r3[1, h, v].astype(jnp.float32)
            )
            acc[0, v, h * half : (h + 1) * half, :] = total
    for b in range(n_enc):
        for v in range(per_rank):
            vg[b, :, v * UNIT : (v + 1) * UNIT] = acc[0, v, 4 * b : 4 * b + 4, :].astype(jnp.bfloat16)
    put_vg = pltpu.make_async_copy(vg, vg_out.at[0, 0], loc.at[4])
    put_vg.start()

    @pl.loop(0, n_enc - 1)
    def _(i):
        other = lax.rem(me + 1 + i, n_enc)
        z_copy(other, other).wait_recv()

    q = z_in[0]
    for s in range(1, n_enc):
        q = q + z_in[s]
    f_own[...] = q

    def f_copy(other, at):
        return remote(f_own, f_in.at[at], f_s.at[other], f_r.at[at], llm=other)

    for d in range(1, n_llm):
        f_copy(lax.rem(group + d, n_llm), group).start()
    f_in[group] = q

    put_vg.wait()
    kv_self.wait()

    @pl.loop(0, n_enc - 1)
    def _(i):
        other = lax.rem(me + 1 + i, n_enc)
        kv_copy(other, other).wait_recv()
        kv_copy(other, me).wait_send()
        cot_copy(other, me).wait_send()
        z_copy(other, me).wait_send()

    for d in range(1, n_tp):
        p_copy(lax.rem(rank + d, n_tp), rank).wait_send()
    for k in range(RING):
        s1_copy(k).wait_send()
    for side in range(2):
        s2_copy(side).wait_send()
        for h in range(2):
            s3_copy(side, h).wait_send()
    for d in range(1, n_llm):
        other = lax.rem(group + d, n_llm)
        q_copy(other, group).wait_send()
        f_copy(other, group).wait_send()
        f_copy(other, other).wait_recv()
    for g in range(n_llm):
        bg_out[g * q_rows : (g + 1) * q_rows, :] = f_in[g]


def per_device(visual, counts, merger_bias, norm_gain, kv_weight, kv_cotangent):
    n_enc, cap, features = visual.shape[2:]
    columns = kv_weight.shape[1]
    n_llm, n_tp = lax.axis_size("llm"), lax.axis_size("tp")
    units = features // UNIT
    per_rank = units // n_tp
    rows = n_enc * cap
    own = features // n_tp
    q_rows = 8 // n_llm
    f32, bf16 = jnp.float32, jnp.bfloat16
    vmem, dma = pltpu.VMEM, pltpu.SemaphoreType.DMA
    any_space = pl.BlockSpec(memory_space=pl.ANY)
    in_vmem = pl.BlockSpec(memory_space=pltpu.VMEM)
    scratch = [
        vmem((n_enc, cap, features), bf16),
        vmem((units, UNIT, columns), bf16),
        vmem((n_enc, cap, columns), bf16),
        vmem((n_enc, cap, columns), bf16),
        vmem((units, rows // 8, 8, UNIT), f32),
        vmem((units, rows // 16, 16, UNIT), bf16),
        vmem((rows // 8, 8, LANES), f32),
        vmem((rows // 8, 8, columns), f32),
        vmem((n_enc, cap, columns), bf16),
        vmem((rows // 8, 8, columns), f32),
        vmem((rows // 8, 8, LANES), f32),
        vmem((RING, per_rank, rows, UNIT), bf16),
        vmem((RING, per_rank, rows, UNIT), bf16),
        vmem((RING, per_rank, rows, UNIT), f32),
        vmem((2, per_rank, rows // 2, UNIT), bf16),
        vmem((2, per_rank, rows // 2, UNIT), bf16),
        vmem((2, 2, per_rank, rows // 2, UNIT), bf16),
        vmem((2, 2, per_rank, rows // 2, UNIT), bf16),
        vmem((n_enc, cap, own), bf16),
        vmem((n_tp, 8, LANES), f32),
        vmem((n_tp, 8, LANES), f32),
        vmem((n_llm, q_rows, LANES), f32),
        vmem((n_llm, q_rows, LANES), f32),
        vmem((q_rows, LANES), f32),
        vmem((n_enc, q_rows, LANES), f32),
        vmem((q_rows, LANES), f32),
        vmem((n_llm, q_rows, LANES), f32),
        *[dma((n_enc,))] * 6,
        *[dma((n_tp,))] * 2,
        *[dma((n_llm,))] * 4,
        *[dma((RING,))] * 2,
        *[dma((2,))] * 2,
        *[dma((2, 2))] * 2,
        dma((5,)),
    ]
    key_values, visual_grad, bias_grad = pl.pallas_call(
        kernel,
        out_shape=(
            jax.ShapeDtypeStruct((1, 1, n_enc, cap, columns), bf16),
            jax.ShapeDtypeStruct((1, 1, n_enc, cap, own), bf16),
            jax.ShapeDtypeStruct((8, LANES), f32),
        ),
        in_specs=[
            pl.BlockSpec(memory_space=pltpu.SMEM),
            in_vmem,
            in_vmem,
            any_space,
            any_space,
            any_space,
        ],
        out_specs=(any_space, any_space, in_vmem),
        scratch_shapes=scratch,
        compiler_params=pltpu.CompilerParams(
            collective_id=0, has_side_effects=True, vmem_limit_bytes=48 << 20
        ),
    )(
        counts,
        merger_bias.reshape(1, features),
        norm_gain.reshape(units, 1, UNIT),
        visual,
        kv_weight.reshape(units, UNIT, columns),
        kv_cotangent,
    )
    return (key_values, visual_grad, bias_grad.reshape(own))


def solution(mesh):
    return jax.shard_map(
        per_device,
        mesh=mesh,
        in_specs=(
            P("enc", "llm", None, None, None),
            P("enc", "llm", None),
            P(),
            P(),
            P(None, "tp"),
            P("enc", "llm", None, None, "tp"),
        ),
        out_specs=(P("enc", "llm", None, None, "tp"), P("enc", "llm", None, None, "tp"), P("tp")),
        check_vma=False,
    )
```

time: 404 us -> 79.1 us (0.20)
  the two profiles are of different devices: /device:TPU:2 before, /device:TPU:1 now
where the time goes in v2:
time: 79.1 us; the launch traced here: 78.3 us
  Pallas kernels  71.1 us (90%)
  local copies, waits for them, and re-layouts  6.52 us (8%)
    pallas_call x1, Pallas kernels, per_device(): pl.pallas_call(kernel, out_shape=(jax.ShapeDtypeStruct((1, 1, n_enc, cap,...  71.1 us
    unnamed x13, local copies, waits for them, and re-layouts  6.52 us

profile of v2, /device:TPU:1, one launch (start us, length us, event | category | flops | bytes accessed | tf_op | source)
XLA Modules:
  0.0 78.3 jit_solution(4863896500936835432)
XLA Ops:
  0.6 0.0 copy-start
  0.6 1.6 %copy-done = bf16[1,1,32,4,8192]{4,3,2,1,0:T(4,128)(2,1)S(1)} copy-done((bf16[1,1,32,4,8192]{4,3,2,1,0:T(4,128)(2,1)S(1)}, bf16[1,1,32,4,8192]{4,3,2,1,0:T(4,128)(2,1)}, u32[]{:S(2)}) %copy-start) | copy-done | bytes 2097176
  2.2 0.0 copy-start.1
  2.2 0.8 %copy-done.1 = bf16[1,1,32,4,256]{4,3,2,1,0:T(4,128)(2,1)S(1)} copy-done((bf16[1,1,32,4,256]{4,3,2,1,0:T(4,128)(2,1)S(1)}, bf16[1,1,32,4,256]{4,3,2,1,0:T(4,128)(2,1)}, u32[]{:S(2)}) %copy-start.1) | copy-done | bytes 65560
  3.1 0.0 copy-start.2
  3.1 0.8 copy-done.2
  3.8 0.0 copy-start.3
  3.8 0.8 copy-done.3
  4.6 0.0 copy-start.4
  4.6 0.7 copy-done.4
  5.2 71.1 %shard_map.85 = (bf16[1,1,32,4,256]{4,3,2,1,0:T(4,128)(2,1)S(1)}, bf16[1,1,32,4,1024]{4,3,2,1,0:T(4,128)(2,1)S(1)}, f32[8,128]{1,0:T(8,128)S(1)}) custom-call(s32[1,1,32]{2,1,0:T(1,128)S(1)} %copy-done.4, f32[1,8192]{1,0:T(1,128)S(1)} %bitcast.4, f32[32,1,256]{2,1,0:T(1,128)S(1)} %bitcast.5, bf16[1,1,32,4,8192]{4,3,2,1,0:T(4,128)(2,1)S(1)} %copy-done, ...), custom_call_target="tpu_custom_call" | custom-call | tf_op jit(solution)/shard_map/pallas_call | solution.py:365
  76.4 0.6 copy.12
  77.0 0.7 copy.13
  77.7 0.6 copy.14
Async XLA Ops:
  0.6 1.6 %copy-start = (bf16[1,1,32,4,8192]{4,3,2,1,0:T(4,128)(2,1)S(1)}, bf16[1,1,32,4,8192]{4,3,2,1,0:T(4,128)(2,1)}, u32[]{:S(2)}) copy-start(bf16[1,1,32,4,8192]{4,3,2,1,0:T(4,128)(2,1)} %vis_hbm.1) | copy-start | bytes 6291460
  2.2 0.8 %copy-start.1 = (bf16[1,1,32,4,256]{4,3,2,1,0:T(4,128)(2,1)S(1)}, bf16[1,1,32,4,256]{4,3,2,1,0:T(4,128)(2,1)}, u32[]{:S(2)}) copy-start(bf16[1,1,32,4,256]{4,3,2,1,0:T(4,128)(2,1)} %cot_hbm.1) | copy-start | bytes 196612
  3.1 0.8 copy-start.2
  3.8 0.8 copy-start.3
  4.6 0.7 copy-start.4

commit v3 on v2

--- a/solution.py
+++ b/solution.py
@@ -24,13 +24,13 @@
 
 
 def kernel(
-    counts, bias, gain, vis_hbm, w_hbm, cot_hbm,
+    counts_hbm, bias_hbm, gain_hbm, vis_hbm, w_hbm, cot_hbm,
     kv_out, vg_out, bg_out,
-    vis, w, cot_own, cot_in, xs, xn, inv, proj, kv_own, masked, coef,
+    counts, bias, gain, vis, w, cot_own, cot_in, hop, xs, xn, inv, proj, kv_own, masked, coef,
     s1, r1, acc, s2, r2, s3, r3, vg,
     p_own, p_in, q_own, q_in, z_own, z_in, f_own, f_in,
     cot_s, cot_r, kv_s, kv_r, z_s, z_r, p_s, p_r, q_s, q_r, f_s, f_r,
-    s1_s, s1_r, s2_s, s2_r, s3_s, s3_r, loc,
+    s1_s, s1_r, s2_s, s2_r, s3_s, s3_r, hop_s, hop_r, loc,
 ):
     n_enc, n_llm = lax.axis_size("enc"), lax.axis_size("llm")
     n_tp = lax.axis_size("tp")
@@ -42,29 +42,42 @@
     rows = n_enc * 4
     pairs = n_enc // 2
 
+    reach = n_enc // 4
+
+    def at_step(d):
+        return lax.rem(me + d + n_enc, n_enc)
+
     barrier = pltpu.get_barrier_semaphore()
 
-    def far(i):
-        step = (i + 1) // 2
-        return lax.rem(me + n_enc // 2 + step * (1 - 2 * lax.rem(i, 2)), n_enc)
-
-    @pl.loop(0, n_enc - 1)
-    def _(i):
-        pl.semaphore_signal(barrier, 1, device_id={"enc": far(i)})
+    @pl.loop(0, reach)
+    def _(i):
+        d = reach - i
+        pl.semaphore_signal(barrier, 1, device_id={"enc": at_step(d)})
+        pl.semaphore_signal(barrier, 1, device_id={"enc": at_step(-d)})
 
     for d in range(1, n_llm):
         pl.semaphore_signal(barrier, 1, device_id={"llm": lax.rem(group + d, n_llm)})
     for d in range(1, n_tp):
         pl.semaphore_signal(barrier, 1, device_id={"tp": lax.rem(rank + d, n_tp)})
 
-    get_vis = pltpu.make_async_copy(vis_hbm.at[0, 0], vis, loc.at[0])
-    get_w = pltpu.make_async_copy(w_hbm, w, loc.at[1])
-    get_cot = pltpu.make_async_copy(cot_hbm.at[0, 0], cot_own, loc.at[2])
-    get_vis.start()
-    get_w.start()
-    get_cot.start()
-
-    get_vis.wait()
+    loads = [
+        pltpu.make_async_copy(src, dst, loc.at[i])
+        for i, (src, dst) in enumerate(
+            (
+                (vis_hbm.at[0, 0], vis),
+                (bias_hbm, bias),
+                (gain_hbm, gain),
+                (cot_hbm.at[0, 0], cot_own),
+                (counts_hbm, counts),
+                (w_hbm, w),
+            )
+        )
+    ]
+    for load in loads:
+        load.start()
+
+    for load in loads[:3]:
+        load.wait()
 
     @pl.loop(0, pairs // 2)
     def _(g):
@@ -85,14 +98,58 @@
             x = xs[u, pl.ds(2 * g, 2)].reshape(16, UNIT)
             xn[u, g] = (x * scale * gain[u]).astype(jnp.bfloat16)
 
-    get_w.wait()
+    for load in loads[3:5]:
+        load.wait()
+    pl.semaphore_wait(barrier, 2 * reach + n_llm - 1 + n_tp - 1)
+
+    def cot_copy(to, at):
+        return remote(cot_own.at[to], cot_in.at[at], cot_s.at[to], cot_r.at[at], enc=to)
+
+    def away(side, d):
+        return at_step(d - 2 * side * d)
+
+    def out_copy(side, q):
+        to = away(side, reach + q)
+        return remote(
+            cot_own.at[to], hop.at[side, q - 1], cot_s.at[to], hop_r.at[side, q - 1],
+            enc=away(side, reach),
+        )
+
+    def on_copy(side, q):
+        origin = away(side, -reach)
+        return remote(
+            hop.at[side, q - 1], cot_in.at[origin], hop_s.at[side, q - 1], cot_r.at[origin],
+            enc=away(side, q),
+        )
+
+    @pl.loop(0, reach)
+    def _(i):
+        out_copy(0, reach - i).start()
+
+        @pl.when(i > 0)
+        def _():
+            out_copy(1, reach - i).start()
+
+    @pl.loop(0, reach)
+    def _(i):
+        for side in range(2):
+            cot_copy(away(side, reach - i), me).start()
+
+    cot_in[me] = cot_own[me]
+
+    loads[5].wait()
     proj[...] = jnp.zeros_like(proj)
-
-    @pl.loop(0, units)
-    def _(u):
-        proj[...] += jnp.dot(
-            xn[u].reshape(rows, UNIT), w[u], preferred_element_type=jnp.float32
-        ).reshape(proj.shape)
+    step_units = 4
+
+    @pl.loop(0, units // step_units)
+    def _(t):
+        total = jnp.zeros((rows, UNIT), jnp.float32)
+        for k in range(step_units):
+            u = t * step_units + k
+            total = total + jnp.dot(
+                xn[u].reshape(rows, UNIT), w[u], preferred_element_type=jnp.float32
+            )
+        proj[...] += total.reshape(proj.shape)
 
     slot = lax.broadcasted_iota(jnp.int32, (4, UNIT), 0)
 
@@ -103,39 +160,38 @@
             kept = jnp.where(slot < counts[0, 0, 2 * i + h], rows4, 0.0)
             kv_own[2 * i + h] = kept.astype(jnp.bfloat16)
 
-    get_cot.wait()
-    pl.semaphore_wait(barrier, n_enc - 1 + n_llm - 1 + n_tp - 1)
-
-    def cot_copy(other, at):
-        return remote(
-            cot_own.at[other], cot_in.at[at], cot_s.at[other], cot_r.at[at], enc=other
-        )
-
-    @pl.loop(0, n_enc - 1)
-    def _(i):
-        cot_copy(far(i), me).start()
-
-    cot_in[me] = cot_own[me]
-
-    @pl.loop(0, n_enc - 1)
-    def _(i):
-        other = lax.rem(me + 1 + i, n_enc)
-        cot_copy(other, other).wait_recv()
-
-    def kv_copy(other, at):
-        return remote(
-            kv_own.at[other], kv_out.at[0, 0, at], kv_s.at[other], kv_r.at[at], enc=other
-        )
-
-    @pl.loop(0, n_enc - 1)
-    def _(i):
-        kv_copy(far(i), me).start()
-
-    kv_self = pltpu.make_async_copy(kv_own.at[me], kv_out.at[0, 0, me], loc.at[3])
+    def kv_copy(to, at):
+        return remote(kv_own.at[to], kv_out.at[0, 0, at], kv_s.at[to], kv_r.at[at], enc=to)
+
+    @pl.loop(0, reach)
+    def _(i):
+        for side in range(2):
+            kv_copy(away(side, reach - i), me).start()
+
+    kv_self = pltpu.make_async_copy(kv_own.at[me], kv_out.at[0, 0, me], loc.at[6])
     kv_self.start()
 
+    @pl.loop(0, reach)
+    def _(i):
+        out_copy(0, reach - i).wait_recv()
+        on_copy(0, reach - i).start()
+
+        @pl.when(i > 0)
+        def _():
+            out_copy(1, reach - i).wait_recv()
+            on_copy(1, reach - i).start()
+
     @pl.loop(0, pairs)
-    def _(i):
+    def _(n):
+        step = (n + 1) // 2
+        i = lax.rem(me // 2 + step * (1 - 2 * lax.rem(n, 2)) + pairs, pairs)
+        for h in range(2):
+            other = 2 * i + h
+
+            @pl.when(other != me)
+            def _():
+                cot_copy(other, other).wait_recv()
+
         for h in range(2):
             got = cot_in[2 * i + h].astype(jnp.float32)
             masked[i, 4 * h : 4 * h + 4, :] = jnp.where(slot < counts[0, 0, 2 * i + h], got, 0.0)
@@ -166,7 +222,6 @@
             part = term(j * per_rank + v)
             s1[k, v] = part.astype(jnp.bfloat16)
             column_sums(j, v, part)
-        s1_copy(k).start()
     for k in order:
         j = lax.rem(chip + k, RING) * 2 + core
         for v in range(per_rank):
@@ -180,6 +235,15 @@
     for d in range(1, n_tp):
         p_copy(lax.rem(rank + d, n_tp), rank).start()
     p_in[rank] = p_own[rank]
+    for k in order:
+        s1_copy(k).start()
+
+    @pl.loop(reach + 1, n_enc // 2)
+    def _(d):
+        for side in range(2):
+            kv_copy(away(side, d), me).start()
+
+    kv_copy(at_step(n_enc // 2), me).start()
 
     half = rows // 2
 
@@ -230,12 +294,6 @@
     q_in[group] = q_own[group]
 
     pair(0)
-    for side, k in ((0, 1), (1, 3)):
-        s2_copy(side).wait_recv()
-        for v in range(per_rank):
-            acc[k, v, side * half : (side + 1) * half, :] += r2[side, v].astype(jnp.float32)
-        fill(s3.at[side, side], k, side)
-        s3_copy(side, side).start()
 
     for d in range(1, n_llm):
         other = lax.rem(group + d, n_llm)
@@ -250,9 +308,17 @@
 
     @pl.loop(0, n_enc - 1)
     def _(i):
-        z_copy(far(i), me).start()
+        step = (i + 1) // 2
+        z_copy(lax.rem(me + n_enc // 2 + step * (1 - 2 * lax.rem(i, 2)), n_enc), me).start()
 
     z_in[me] = q
+
+    for side, k in ((0, 1), (1, 3)):
+        s2_copy(side).wait_recv()
+        for v in range(per_rank):
+            acc[k, v, side * half : (side + 1) * half, :] += r2[side, v].astype(jnp.float32)
+        fill(s3.at[side, side], k, side)
+        s3_copy(side, side).start()
 
     for h in range(2):
         for side in range(2):
@@ -265,7 +331,7 @@
     for b in range(n_enc):
         for v in range(per_rank):
             vg[b, :, v * UNIT : (v + 1) * UNIT] = acc[0, v, 4 * b : 4 * b + 4, :].astype(jnp.bfloat16)
-    put_vg = pltpu.make_async_copy(vg, vg_out.at[0, 0], loc.at[4])
+    put_vg = pltpu.make_async_copy(vg, vg_out.at[0, 0], loc.at[7])
     put_vg.start()
 
     @pl.loop(0, n_enc - 1)
@@ -295,6 +361,14 @@
         kv_copy(other, me).wait_send()
         cot_copy(other, me).wait_send()
         z_copy(other, me).wait_send()
+
+    @pl.loop(0, reach)
+    def _(i):
+        on_copy(0, reach - i).wait_send()
+
+        @pl.when(i > 0)
+        def _():
+            on_copy(1, reach - i).wait_send()
 
     for d in range(1, n_tp):
         p_copy(lax.rem(rank + d, n_tp), rank).wait_send()
@@ -325,12 +399,18 @@
     f32, bf16 = jnp.float32, jnp.bfloat16
     vmem, dma = pltpu.VMEM, pltpu.SemaphoreType.DMA
     any_space = pl.BlockSpec(memory_space=pl.ANY)
+    in_hbm = any_space
+    reach = n_enc // 4
     in_vmem = pl.BlockSpec(memory_space=pltpu.VMEM)
     scratch = [
+        pltpu.SMEM((1, 1, n_enc), jnp.int32),
+        vmem((1, features), f32),
+        vmem((units, 1, UNIT), f32),
         vmem((n_enc, cap, features), bf16),
         vmem((units, UNIT, columns), bf16),
         vmem((n_enc, cap, columns), bf16),
         vmem((n_enc, cap, columns), bf16),
+        vmem((2, reach, cap, columns), bf16),
         vmem((units, rows // 8, 8, UNIT), f32),
         vmem((units, rows // 16, 16, UNIT), bf16),
         vmem((rows // 8, 8, LANES), f32),
@@ -360,7 +440,8 @@
         *[dma((RING,))] * 2,
         *[dma((2,))] * 2,
         *[dma((2, 2))] * 2,
-        dma((5,)),
+        *[dma((2, reach))] * 2,
+        dma((8,)),
     ]
     key_values, visual_grad, bias_grad = pl.pallas_call(
         kernel,
@@ -369,18 +450,11 @@
             jax.ShapeDtypeStruct((1, 1, n_enc, cap, own), bf16),
             jax.ShapeDtypeStruct((8, LANES), f32),
         ),
-        in_specs=[
-            pl.BlockSpec(memory_space=pltpu.SMEM),
-            in_vmem,
-            in_vmem,
-            any_space,
-            any_space,
-            any_space,
-        ],
+        in_specs=[in_hbm] * 6,
         out_specs=(any_space, any_space, in_vmem),
         scratch_shapes=scratch,
         compiler_params=pltpu.CompilerParams(
-            collective_id=0, has_side_effects=True, vmem_limit_bytes=48 << 20
+            collective_id=0, has_side_effects=True, vmem_limit_bytes=67043328
         ),
     )(
         counts,

time: 79.1 us -> 69.7 us (0.88)
  Pallas kernels: 71.1 us -> 64.1 us
  local copies, waits for them, and re-layouts: 6.52 us -> 4.51 us
    pallas_call x1, Pallas kernels: 71.1 us -> 64.1 us  [per_device(): pl.pallas_call(kernel, out_shape=(jax.ShapeDtypeStruct((1, 1, n_enc, cap,...]
    unnamed x13 -> x3, local copies, waits for them, and re-layouts: 6.52 us -> 4.51 us
where the time goes in v3:
time: 69.7 us; the launch traced here: 69.3 us
  Pallas kernels  64.1 us (92%)
  local copies, waits for them, and re-layouts  4.51 us (6%)
    pallas_call x1, Pallas kernels, per_device(): pl.pallas_call(kernel, out_shape=(jax.ShapeDtypeStruct((1, 1, n_enc, cap,...  64.1 us
    unnamed x3, local copies, waits for them, and re-layouts  4.51 us

profile of v3, /device:TPU:1, one launch (start us, length us, event | category | flops | bytes accessed | tf_op | source)
XLA Modules:
  0.0 69.3 jit_solution(11685127469362731019)
XLA Ops:
  0.6 64.1 %shard_map.85 = (bf16[1,1,32,4,256]{4,3,2,1,0:T(4,128)(2,1)}, bf16[1,1,32,4,1024]{4,3,2,1,0:T(4,128)(2,1)}, f32[8,128]{1,0:T(8,128)}) custom-call(s32[1,1,32]{2,1,0:T(1,128)} %counts_hbm.1, f32[1,8192]{1,0:T(1,128)} %bitcast.5, f32[32,1,256]{2,1,0:T(1,128)} %bitcast.6, bf16[1,1,32,4,8192]{4,3,2,1,0:T(4,128)(2,1)} %vis_hbm.1, bf16[32,256,256]{2,1,0:T(8,128)(2,1)} %bitcast.4, ...), custom_call_target="tpu_custom_call" | custom-call | tf_op jit(solution)/shard_map/pallas_call | solution.py:446
  64.7 1.5 %copy.12 = bf16[1,1,32,4,256]{4,3,2,1,0:T(4,128)(2,1)} copy(bf16[1,1,32,4,256]{4,3,2,1,0:T(4,128)(2,1)} %get-tuple-element.12) | data formatting | bytes 131072
  66.2 1.7 %copy.13 = bf16[1,1,32,4,1024]{4,3,2,1,0:T(4,128)(2,1)} copy(bf16[1,1,32,4,1024]{4,3,2,1,0:T(4,128)(2,1)} %get-tuple-element.13) | data formatting | bytes 524288
  68.0 1.3 %copy.14 = f32[1024]{0:T(1024)} copy(f32[1024]{0:T(1024)} %bitcast.7) | data formatting | bytes 8192

commit v4 on v3

--- a/solution.py
+++ b/solution.py
@@ -28,8 +28,8 @@
     kv_out, vg_out, bg_out,
     counts, bias, gain, vis, w, cot_own, cot_in, hop, xs, xn, inv, proj, kv_own, masked, coef,
     s1, r1, acc, s2, r2, s3, r3, vg,
-    p_own, p_in, q_own, q_in, z_own, z_in, f_own, f_in,
-    cot_s, cot_r, kv_s, kv_r, z_s, z_r, p_s, p_r, q_s, q_r, f_s, f_r,
+    p_own, p_in, z_own, z_in, f_own, kv_hop,
+    cot_s, cot_r, kv_s, kv_r, z_s, z_r, p_s, p_r, f_s, f_r, kv_hop_s, kv_hop_r,
     s1_s, s1_r, s2_s, s2_r, s3_s, s3_r, hop_s, hop_r, loc,
 ):
     n_enc, n_llm = lax.axis_size("enc"), lax.axis_size("llm")
@@ -55,10 +55,17 @@
         pl.semaphore_signal(barrier, 1, device_id={"enc": at_step(d)})
         pl.semaphore_signal(barrier, 1, device_id={"enc": at_step(-d)})
 
-    for d in range(1, n_llm):
-        pl.semaphore_signal(barrier, 1, device_id={"llm": lax.rem(group + d, n_llm)})
-    for d in range(1, n_tp):
-        pl.semaphore_signal(barrier, 1, device_id={"tp": lax.rem(rank + d, n_tp)})
+    plane = n_llm * n_tp
+    q_rows = 8 // n_llm
+
+    def in_plane(i):
+        place = lax.rem(group * n_tp + rank + 1 + i, plane)
+        return place // n_tp, lax.rem(place, n_tp)
+
+    @pl.loop(0, plane - 1)
+    def _(i):
+        g, t = in_plane(i)
+        pl.semaphore_signal(barrier, 1, device_id={"llm": g, "tp": t})
 
     loads = [
         pltpu.make_async_copy(src, dst, loc.at[i])
@@ -100,7 +107,7 @@
 
     for load in loads[3:5]:
         load.wait()
-    pl.semaphore_wait(barrier, 2 * reach + n_llm - 1 + n_tp - 1)
+    pl.semaphore_wait(barrier, 2 * reach + plane - 1)
 
     def cot_copy(to, at):
         return remote(cot_own.at[to], cot_in.at[at], cot_s.at[to], cot_r.at[at], enc=to)
@@ -163,6 +170,28 @@
     def kv_copy(to, at):
         return remote(kv_own.at[to], kv_out.at[0, 0, at], kv_s.at[to], kv_r.at[at], enc=to)
 
+    def kv_out_copy(side, q):
+        to = away(side, reach + q)
+        return remote(
+            kv_own.at[to], kv_hop.at[side, q - 1], kv_s.at[to], kv_hop_r.at[side, q - 1],
+            enc=away(side, reach),
+        )
+
+    def kv_on_copy(side, q):
+        origin = away(side, -reach)
+        return remote(
+            kv_hop.at[side, q - 1], kv_out.at[0, 0, origin], kv_hop_s.at[side, q - 1],
+            kv_r.at[origin], enc=away(side, q),
+        )
+
+    @pl.loop(0, reach)
+    def _(i):
+        kv_out_copy(0, reach - i).start()
+
+        @pl.when(i > 0)
+        def _():
+            kv_out_copy(1, reach - i).start()
+
     @pl.loop(0, reach)
     def _(i):
         for side in range(2):
@@ -210,7 +239,8 @@
     def column_sums(j, v, part):
         total = jnp.sum(part, axis=0, keepdims=True)
         for k in range(UNIT // LANES):
-            p_own[j, pl.ds(v * (UNIT // LANES) + k, 1), :] = total[:, k * LANES : (k + 1) * LANES]
+            g, r = divmod(v * (UNIT // LANES) + k, q_rows)
+            p_own[g, j, r : r + 1, :] = total[:, k * LANES : (k + 1) * LANES]
 
     def s1_copy(k):
         return remote(s1.at[k], r1.at[k], s1_s.at[k], s1_r.at[k], tp=rank + 1 - 2 * core)
@@ -229,21 +259,28 @@
             acc[k, v] = part
             column_sums(j, v, part)
 
-    def p_copy(other, at):
-        return remote(p_own.at[other], p_in.at[at], p_s.at[other], p_r.at[at], tp=other)
-
-    for d in range(1, n_tp):
-        p_copy(lax.rem(rank + d, n_tp), rank).start()
-    p_in[rank] = p_own[rank]
+    def p_copy(g, t, at_g, at_t):
+        return remote(
+            p_own.at[g, t], p_in.at[at_g, at_t], p_s.at[g, t], p_r.at[at_g, at_t], llm=g, tp=t
+        )
+
+    @pl.loop(0, plane - 1)
+    def _(i):
+        p_copy(*in_plane(i), group, rank).start()
+
+    p_in[group, rank] = p_own[group, rank]
     for k in order:
         s1_copy(k).start()
 
-    @pl.loop(reach + 1, n_enc // 2)
-    def _(d):
-        for side in range(2):
-            kv_copy(away(side, d), me).start()
-
-    kv_copy(at_step(n_enc // 2), me).start()
+    @pl.loop(0, reach)
+    def _(i):
+        kv_out_copy(0, reach - i).wait_recv()
+        kv_on_copy(0, reach - i).start()
+
+        @pl.when(i > 0)
+        def _():
+            kv_out_copy(1, reach - i).wait_recv()
+            kv_on_copy(1, reach - i).start()
 
     half = rows // 2
 
@@ -276,31 +313,17 @@
         fill(s3.at[side, 1 - side], k, 1 - side)
         s3_copy(side, 1 - side).start()
 
-    for d in range(1, n_tp):
-        other = lax.rem(rank + d, n_tp)
-        p_copy(other, other).wait_recv()
-    q = p_in[0]
-    for t in range(1, n_tp):
-        q = q + p_in[t]
-    q_rows = 8 // n_llm
+    pair(0)
+
+    @pl.loop(0, plane - 1)
+    def _(i):
+        g, t = in_plane(i)
+        p_copy(g, t, g, t).wait_recv()
+
+    q = jnp.zeros((q_rows, LANES), jnp.float32)
     for g in range(n_llm):
-        q_own[g] = q[g * q_rows : (g + 1) * q_rows, :]
-
-    def q_copy(other, at):
-        return remote(q_own.at[other], q_in.at[at], q_s.at[other], q_r.at[at], llm=other)
-
-    for d in range(1, n_llm):
-        q_copy(lax.rem(group + d, n_llm), group).start()
-    q_in[group] = q_own[group]
-
-    pair(0)
-
-    for d in range(1, n_llm):
-        other = lax.rem(group + d, n_llm)
-        q_copy(other, other).wait_recv()
-    q = q_in[0]
-    for g in range(1, n_llm):
-        q = q + q_in[g]
+        for t in range(n_tp):
+            q = q + p_in[g, t]
     z_own[...] = q
 
     def z_copy(other, at):
@@ -345,14 +368,16 @@
     f_own[...] = q
 
     def f_copy(other, at):
-        return remote(f_own, f_in.at[at], f_s.at[other], f_r.at[at], llm=other)
+        return remote(f_own, bg_out.at[at], f_s.at[other], f_r.at[at], llm=other)
 
     for d in range(1, n_llm):
         f_copy(lax.rem(group + d, n_llm), group).start()
-    f_in[group] = q
+    put_f = pltpu.make_async_copy(f_own, bg_out.at[group], loc.at[8])
+    put_f.start()
 
     put_vg.wait()
     kv_self.wait()
+    put_f.wait()
 
     @pl.loop(0, n_enc - 1)
     def _(i):
@@ -365,13 +390,17 @@
     @pl.loop(0, reach)
     def _(i):
         on_copy(0, reach - i).wait_send()
+        kv_on_copy(0, reach - i).wait_send()
 
         @pl.when(i > 0)
         def _():
             on_copy(1, reach - i).wait_send()
-
-    for d in range(1, n_tp):
-        p_copy(lax.rem(rank + d, n_tp), rank).wait_send()
+            kv_on_copy(1, reach - i).wait_send()
+
+    @pl.loop(0, plane - 1)
+    def _(i):
+        p_copy(*in_plane(i), group, rank).wait_send()
+
     for k in range(RING):
         s1_copy(k).wait_send()
     for side in range(2):
@@ -380,11 +409,19 @@
             s3_copy(side, h).wait_send()
     for d in range(1, n_llm):
         other = lax.rem(group + d, n_llm)
-        q_copy(other, group).wait_send()
         f_copy(other, group).wait_send()
         f_copy(other, other).wait_recv()
-    for g in range(n_llm):
-        bg_out[g * q_rows : (g + 1) * q_rows, :] = f_in[g]
+
+
+def write_back(kv, vg, bg, kv_out, vg_out, bg_out, sems):
+    puts = [
+        pltpu.make_async_copy(src, dst, sems.at[i])
+        for i, (src, dst) in enumerate(((vg, vg_out), (kv, kv_out), (bg, bg_out)))
+    ]
+    for put in puts:
+        put.start()
+    for put in puts:
+        put.wait()
 
 
 def per_device(visual, counts, merger_bias, norm_gain, kv_weight, kv_cotangent):
@@ -401,7 +438,6 @@
     any_space = pl.BlockSpec(memory_space=pl.ANY)
     in_hbm = any_space
     reach = n_enc // 4
-    in_vmem = pl.BlockSpec(memory_space=pltpu.VMEM)
     scratch = [
         pltpu.SMEM((1, 1, n_enc), jnp.int32),
         vmem((1, features), f32),
@@ -426,44 +462,56 @@
         vmem((2, 2, per_rank, rows // 2, UNIT), bf16),
         vmem((2, 2, per_rank, rows // 2, UNIT), bf16),
         vmem((n_enc, cap, own), bf16),
-        vmem((n_tp, 8, LANES), f32),
-        vmem((n_tp, 8, LANES), f32),
-        vmem((n_llm, q_rows, LANES), f32),
-        vmem((n_llm, q_rows, LANES), f32),
+        vmem((n_llm, n_tp, q_rows, LANES), f32),
+        vmem((n_llm, n_tp, q_rows, LANES), f32),
         vmem((q_rows, LANES), f32),
         vmem((n_enc, q_rows, LANES), f32),
         vmem((q_rows, LANES), f32),
-        vmem((n_llm, q_rows, LANES), f32),
+        vmem((2, reach, cap, columns), bf16),
         *[dma((n_enc,))] * 6,
-        *[dma((n_tp,))] * 2,
-        *[dma((n_llm,))] * 4,
+        *[dma((n_llm, n_tp))] * 2,
+        *[dma((n_llm,))] * 2,
+        *[dma((2, reach))] * 2,
         *[dma((RING,))] * 2,
         *[dma((2,))] * 2,
         *[dma((2, 2))] * 2,
         *[dma((2, reach))] * 2,
-        dma((8,)),
+        dma((9,)),
     ]
-    key_values, visual_grad, bias_grad = pl.pallas_call(
+    results = (
+        jax.ShapeDtypeStruct((1, 1, n_enc, cap, columns), bf16),
+        jax.ShapeDtypeStruct((1, 1, n_enc, cap, own), bf16),
+        jax.ShapeDtypeStruct((n_llm, q_rows, LANES), f32),
+    )
+    parts = pl.pallas_call(
         kernel,
-        out_shape=(
-            jax.ShapeDtypeStruct((1, 1, n_enc, cap, columns), bf16),
-            jax.ShapeDtypeStruct((1, 1, n_enc, cap, own), bf16),
-            jax.ShapeDtypeStruct((8, LANES), f32),
-        ),
+        out_shape=results,
         in_specs=[in_hbm] * 6,
-        out_specs=(any_space, any_space, in_vmem),
+        out_specs=[any_space] * 3,
         scratch_shapes=scratch,
         compiler_params=pltpu.CompilerParams(
-            collective_id=0, has_side_effects=True, vmem_limit_bytes=67043328
+            collective_id=0, has_side_effects=True, vmem_limit_bytes=48 << 20
         ),
     )(
-        counts,
-        merger_bias.reshape(1, features),
-        norm_gain.reshape(units, 1, UNIT),
-        visual,
-        kv_weight.reshape(units, UNIT, columns),
-        kv_cotangent,
+        *[
+            pltpu.with_memory_space_constraint(value, pltpu.HBM)
+            for value in (
+                counts,
+                merger_bias.reshape(1, features),
+                norm_gain.reshape(units, 1, UNIT),
+                visual,
+                kv_weight.reshape(units, UNIT, columns),
+                kv_cotangent,
+            )
+        ]
     )
+    key_values, visual_grad, bias_grad = pl.pallas_call(
+        write_back,
+        out_shape=results,
+        in_specs=[any_space] * 3,
+        out_specs=[any_space] * 3,
+        scratch_shapes=[dma((3,))],
+    )(*[pltpu.with_memory_space_constraint(part, pltpu.VMEM) for part in parts])
     return (key_values, visual_grad, bias_grad.reshape(own))
 
 

time: 69.7 us -> 66.7 us (0.957)
  local copies, waits for them, and re-layouts: 4.51 us -> 0 us
  Pallas kernels: 64.1 us -> 65.8 us
    unnamed x3 -> x0, local copies, waits for them, and re-layouts: 4.51 us -> none
    pallas_call x1 -> x2, Pallas kernels: 64.1 us -> 65.8 us  [the longest x1 65.1 us: per_device(): pl.pallas_call(kernel, out_shape=results, in_specs=[in_hbm] * 6, out_spec...]
where the time goes in v4:
time: 66.7 us; the launch traced here: 66.4 us
  Pallas kernels  65.8 us (99%)
    pallas_call x1, Pallas kernels, per_device(): pl.pallas_call(kernel, out_shape=results, in_specs=[in_hbm] * 6, out_spec...  65.1 us

profile of v4, /device:TPU:1, one launch (start us, length us, event | category | flops | bytes accessed | tf_op | source)
XLA Modules:
  0.0 66.4 jit_solution(617815915482376245)
XLA Ops:
  0.6 65.1 %shard_map.85 = (bf16[1,1,32,4,256]{4,3,2,1,0:T(4,128)(2,1)S(1)}, bf16[1,1,32,4,1024]{4,3,2,1,0:T(4,128)(2,1)S(1)}, f32[4,2,128]{2,1,0:T(2,128)S(1)}) custom-call(s32[1,1,32]{2,1,0:T(1,128)} %counts_hbm.1, f32[1,8192]{1,0:T(1,128)} %bitcast.5, f32[32,1,256]{2,1,0:T(1,128)} %bitcast.6, bf16[1,1,32,4,8192]{4,3,2,1,0:T(4,128)(2,1)} %vis_hbm.1, ...), custom_call_target="tpu_custom_call" | custom-call | tf_op jit(solution)/shard_map/pallas_call | solution.py:486
  65.7 0.7 %shard_map.86 = (bf16[1,1,32,4,256]{4,3,2,1,0:T(4,128)(2,1)}, bf16[1,1,32,4,1024]{4,3,2,1,0:T(4,128)(2,1)}, f32[4,2,128]{2,1,0:T(2,128)}) custom-call(bf16[1,1,32,4,256]{4,3,2,1,0:T(4,128)(2,1)S(1)} %get-tuple-element.9.kv, bf16[1,1,32,4,1024]{4,3,2,1,0:T(4,128)(2,1)S(1)} %get-tuple-element.10.vg, f32[4,2,128]{2,1,0:T(2,128)S(1)} %get-tuple-element.11.bg), custom_call_target="tpu_custom_call" | custom-call | tf_op jit(solution)/shard_map/pallas_call | solution.py:508

commit v5 on v4

--- a/solution.py
+++ b/solution.py
@@ -167,6 +167,16 @@
             kept = jnp.where(slot < counts[0, 0, 2 * i + h], rows4, 0.0)
             kv_own[2 * i + h] = kept.astype(jnp.bfloat16)
 
+    @pl.loop(0, reach)
+    def _(i):
+        out_copy(0, reach - i).wait_recv()
+        on_copy(0, reach - i).start()
+
+        @pl.when(i > 0)
+        def _():
+            out_copy(1, reach - i).wait_recv()
+            on_copy(1, reach - i).start()
+
     def kv_copy(to, at):
         return remote(kv_own.at[to], kv_out.at[0, 0, at], kv_s.at[to], kv_r.at[at], enc=to)
 
@@ -199,16 +209,6 @@
 
     kv_self = pltpu.make_async_copy(kv_own.at[me], kv_out.at[0, 0, me], loc.at[6])
     kv_self.start()
-
-    @pl.loop(0, reach)
-    def _(i):
-        out_copy(0, reach - i).wait_recv()
-        on_copy(0, reach - i).start()
-
-        @pl.when(i > 0)
-        def _():
-            out_copy(1, reach - i).wait_recv()
-            on_copy(1, reach - i).start()
 
     @pl.loop(0, pairs)
     def _(n):
@@ -271,6 +271,27 @@
     p_in[group, rank] = p_own[group, rank]
     for k in order:
         s1_copy(k).start()
+
+    @pl.loop(0, plane - 1)
+    def _(i):
+        g, t = in_plane(i)
+        p_copy(g, t, g, t).wait_recv()
+
+    q = jnp.zeros((q_rows, LANES), jnp.float32)
+    for g in range(n_llm):
+        for t in range(n_tp):
+            q = q + p_in[g, t]
+    z_own[...] = q
+
+    def z_copy(other, at):
+        return remote(z_own, z_in.at[at], z_s.at[other], z_r.at[at], enc=other)
+
+    @pl.loop(0, n_enc - 1)
+    def _(i):
+        step = (i + 1) // 2
+        z_copy(lax.rem(me + n_enc // 2 + step * (1 - 2 * lax.rem(i, 2)), n_enc), me).start()
+
+    z_in[me] = q
 
     @pl.loop(0, reach)
     def _(i):
@@ -314,27 +335,6 @@
         s3_copy(side, 1 - side).start()
 
     pair(0)
-
-    @pl.loop(0, plane - 1)
-    def _(i):
-        g, t = in_plane(i)
-        p_copy(g, t, g, t).wait_recv()
-
-    q = jnp.zeros((q_rows, LANES), jnp.float32)
-    for g in range(n_llm):
-        for t in range(n_tp):
-            q = q + p_in[g, t]
-    z_own[...] = q
-
-    def z_copy(other, at):
-        return remote(z_own, z_in.at[at], z_s.at[other], z_r.at[at], enc=other)
-
-    @pl.loop(0, n_enc - 1)
-    def _(i):
-        step = (i + 1) // 2
-        z_copy(lax.rem(me + n_enc // 2 + step * (1 - 2 * lax.rem(i, 2)), n_enc), me).start()
-
-    z_in[me] = q
 
     for side, k in ((0, 1), (1, 3)):
         s2_copy(side).wait_recv()

time: 66.7 us -> 66.7 us (level)
  no operation moved by 1% of the time
where the time goes in v5:
time: 66.7 us; the launch traced here: 66.5 us
  Pallas kernels  65.9 us (99%)
    pallas_call x1, Pallas kernels, per_device(): pl.pallas_call(kernel, out_shape=results, in_specs=[in_hbm] * 6, out_spec...  65.1 us

profile of v5, /device:TPU:1, one launch (start us, length us, event | category | flops | bytes accessed | tf_op | source)
XLA Modules:
  0.0 66.5 jit_solution(8178548714414507313)
XLA Ops:
  0.6 65.1 %shard_map.85 = (bf16[1,1,32,4,256]{4,3,2,1,0:T(4,128)(2,1)S(1)}, bf16[1,1,32,4,1024]{4,3,2,1,0:T(4,128)(2,1)S(1)}, f32[4,2,128]{2,1,0:T(2,128)S(1)}) custom-call(s32[1,1,32]{2,1,0:T(1,128)} %counts_hbm.1, f32[1,8192]{1,0:T(1,128)} %bitcast.5, f32[32,1,256]{2,1,0:T(1,128)} %bitcast.6, bf16[1,1,32,4,8192]{4,3,2,1,0:T(4,128)(2,1)} %vis_hbm.1, ...), custom_call_target="tpu_custom_call" | custom-call | tf_op jit(solution)/shard_map/pallas_call | solution.py:486
  65.8 0.7 %shard_map.86 = (bf16[1,1,32,4,256]{4,3,2,1,0:T(4,128)(2,1)}, bf16[1,1,32,4,1024]{4,3,2,1,0:T(4,128)(2,1)}, f32[4,2,128]{2,1,0:T(2,128)}) custom-call(bf16[1,1,32,4,256]{4,3,2,1,0:T(4,128)(2,1)S(1)} %get-tuple-element.9.kv, bf16[1,1,32,4,1024]{4,3,2,1,0:T(4,128)(2,1)S(1)} %get-tuple-element.10.vg, f32[4,2,128]{2,1,0:T(2,128)S(1)} %get-tuple-element.11.bg), custom_call_target="tpu_custom_call" | custom-call | tf_op jit(solution)/shard_map/pallas_call | solution.py:508

commit v6 on v5

--- a/solution.py
+++ b/solution.py
@@ -23,6 +23,10 @@
     )
 
 
+def wide(v):
+    return jnp.concatenate([v] * (UNIT // LANES), axis=1)
+
+
 def kernel(
     counts_hbm, bias_hbm, gain_hbm, vis_hbm, w_hbm, cot_hbm,
     kv_out, vg_out, bg_out,
@@ -30,7 +34,7 @@
     s1, r1, acc, s2, r2, s3, r3, vg,
     p_own, p_in, z_own, z_in, f_own, kv_hop,
     cot_s, cot_r, kv_s, kv_r, z_s, z_r, p_s, p_r, f_s, f_r, kv_hop_s, kv_hop_r,
-    s1_s, s1_r, s2_s, s2_r, s3_s, s3_r, hop_s, hop_r, loc,
+    s1_s, s1_r, s2_s, s2_r, s3_s, s3_r, hop_s, hop_r, loc, deep,
 ):
     n_enc, n_llm = lax.axis_size("enc"), lax.axis_size("llm")
     n_tp = lax.axis_size("tp")
@@ -42,7 +46,8 @@
     rows = n_enc * 4
     pairs = n_enc // 2
 
-    reach = n_enc // 4
+    far = hop.shape[1]
+    reach = n_enc // 2 - far
 
     def at_step(d):
         return lax.rem(me + d + n_enc, n_enc)
@@ -100,7 +105,7 @@
                 squares = squares + x * x
             mean = jnp.sum(squares, axis=1, keepdims=True) * (1.0 / features)
             inv[i] = jnp.broadcast_to(lax.rsqrt(mean + 1e-06), (8, LANES))
-        scale = inv[pl.ds(2 * g, 2)].reshape(16, LANES)[:, :1]
+        scale = wide(inv[pl.ds(2 * g, 2)].reshape(16, LANES))
         for u in range(units):
             x = xs[u, pl.ds(2 * g, 2)].reshape(16, UNIT)
             xn[u, g] = (x * scale * gain[u]).astype(jnp.bfloat16)
@@ -108,6 +113,8 @@
     for load in loads[3:5]:
         load.wait()
     pl.semaphore_wait(barrier, 2 * reach + plane - 1)
+    for side in range(2):
+        pl.semaphore_signal(deep, 1, device_id={"enc": at_step(reach - 2 * side * reach)})
 
     def cot_copy(to, at):
         return remote(cot_own.at[to], cot_in.at[at], cot_s.at[to], cot_r.at[at], enc=to)
@@ -129,13 +136,13 @@
             enc=away(side, q),
         )
 
-    @pl.loop(0, reach)
-    def _(i):
-        out_copy(0, reach - i).start()
+    @pl.loop(0, far)
+    def _(i):
+        out_copy(0, far - i).start()
 
         @pl.when(i > 0)
         def _():
-            out_copy(1, reach - i).start()
+            out_copy(1, far - i).start()
 
     @pl.loop(0, reach)
     def _(i):
@@ -167,15 +174,17 @@
             kept = jnp.where(slot < counts[0, 0, 2 * i + h], rows4, 0.0)
             kv_own[2 * i + h] = kept.astype(jnp.bfloat16)
 
-    @pl.loop(0, reach)
-    def _(i):
-        out_copy(0, reach - i).wait_recv()
-        on_copy(0, reach - i).start()
+    pl.semaphore_wait(deep, 2)
+
+    @pl.loop(0, far)
+    def _(i):
+        out_copy(0, far - i).wait_recv()
+        on_copy(0, far - i).start()
 
         @pl.when(i > 0)
         def _():
-            out_copy(1, reach - i).wait_recv()
-            on_copy(1, reach - i).start()
+            out_copy(1, far - i).wait_recv()
+            on_copy(1, far - i).start()
 
     def kv_copy(to, at):
         return remote(kv_own.at[to], kv_out.at[0, 0, at], kv_s.at[to], kv_r.at[at], enc=to)
@@ -194,13 +203,13 @@
             kv_r.at[origin], enc=away(side, q),
         )
 
-    @pl.loop(0, reach)
-    def _(i):
-        kv_out_copy(0, reach - i).start()
+    @pl.loop(0, far)
+    def _(i):
+        kv_out_copy(0, far - i).start()
 
         @pl.when(i > 0)
         def _():
-            kv_out_copy(1, reach - i).start()
+            kv_out_copy(1, far - i).start()
 
     @pl.loop(0, reach)
     def _(i):
@@ -232,8 +241,7 @@
         grad = lax.dot_general(
             cot16, w[u], (((1,), (1,)), ((), ())), preferred_element_type=jnp.float32
         )
-        a = inv[...].reshape(rows, LANES)[:, :1]
-        b = coef[...].reshape(rows, LANES)[:, :1]
+        a, b = wide(inv[...].reshape(rows, LANES)), wide(coef[...].reshape(rows, LANES))
         return a * gain[u] * grad - xs[u].reshape(rows, UNIT) * b
 
     def column_sums(j, v, part):
@@ -293,15 +301,15 @@
 
     z_in[me] = q
 
-    @pl.loop(0, reach)
-    def _(i):
-        kv_out_copy(0, reach - i).wait_recv()
-        kv_on_copy(0, reach - i).start()
+    @pl.loop(0, far)
+    def _(i):
+        kv_out_copy(0, far - i).wait_recv()
+        kv_on_copy(0, far - i).start()
 
         @pl.when(i > 0)
         def _():
-            kv_out_copy(1, reach - i).wait_recv()
-            kv_on_copy(1, reach - i).start()
+            kv_out_copy(1, far - i).wait_recv()
+            kv_on_copy(1, far - i).start()
 
     half = rows // 2
 
@@ -387,15 +395,15 @@
         cot_copy(other, me).wait_send()
         z_copy(other, me).wait_send()
 
-    @pl.loop(0, reach)
-    def _(i):
-        on_copy(0, reach - i).wait_send()
-        kv_on_copy(0, reach - i).wait_send()
+    @pl.loop(0, far)
+    def _(i):
+        on_copy(0, far - i).wait_send()
+        kv_on_copy(0, far - i).wait_send()
 
         @pl.when(i > 0)
         def _():
-            on_copy(1, reach - i).wait_send()
-            kv_on_copy(1, reach - i).wait_send()
+            on_copy(1, far - i).wait_send()
+            kv_on_copy(1, far - i).wait_send()
 
     @pl.loop(0, plane - 1)
     def _(i):
@@ -437,7 +445,7 @@
     vmem, dma = pltpu.VMEM, pltpu.SemaphoreType.DMA
     any_space = pl.BlockSpec(memory_space=pl.ANY)
     in_hbm = any_space
-    reach = n_enc // 4
+    far = n_enc // 2 - (n_enc // 2 + 2) // 3
     scratch = [
         pltpu.SMEM((1, 1, n_enc), jnp.int32),
         vmem((1, features), f32),
@@ -446,7 +454,7 @@
         vmem((units, UNIT, columns), bf16),
         vmem((n_enc, cap, columns), bf16),
         vmem((n_enc, cap, columns), bf16),
-        vmem((2, reach, cap, columns), bf16),
+        vmem((2, far, cap, columns), bf16),
         vmem((units, rows // 8, 8, UNIT), f32),
         vmem((units, rows // 16, 16, UNIT), bf16),
         vmem((rows // 8, 8, LANES), f32),
@@ -467,16 +475,17 @@
         vmem((q_rows, LANES), f32),
         vmem((n_enc, q_rows, LANES), f32),
         vmem((q_rows, LANES), f32),
-        vmem((2, reach, cap, columns), bf16),
+        vmem((2, far, cap, columns), bf16),
         *[dma((n_enc,))] * 6,
         *[dma((n_llm, n_tp))] * 2,
         *[dma((n_llm,))] * 2,
-        *[dma((2, reach))] * 2,
+        *[dma((2, far))] * 2,
         *[dma((RING,))] * 2,
         *[dma((2,))] * 2,
         *[dma((2, 2))] * 2,
-        *[dma((2, reach))] * 2,
+        *[dma((2, far))] * 2,
         dma((9,)),
+        pltpu.SemaphoreType.REGULAR,
     ]
     results = (
         jax.ShapeDtypeStruct((1, 1, n_enc, cap, columns), bf16),

time: 66.7 us -> 66.7 us (level)
  no operation moved by 1% of the time
where the time goes in v6:
time: 66.7 us; the launch traced here: 66.6 us
  Pallas kernels  65.9 us (99%)
    pallas_call x1, Pallas kernels, per_device(): pl.pallas_call(kernel, out_shape=results, in_specs=[in_hbm] * 6, out_spec...  65.2 us

profile of v6, /device:TPU:1, one launch (start us, length us, event | category | flops | bytes accessed | tf_op | source)
XLA Modules:
  0.0 66.6 jit_solution(505542223949788136)
XLA Ops:
  0.6 65.2 %shard_map.85 = (bf16[1,1,32,4,256]{4,3,2,1,0:T(4,128)(2,1)S(1)}, bf16[1,1,32,4,1024]{4,3,2,1,0:T(4,128)(2,1)S(1)}, f32[4,2,128]{2,1,0:T(2,128)S(1)}) custom-call(s32[1,1,32]{2,1,0:T(1,128)} %counts_hbm.1, f32[1,8192]{1,0:T(1,128)} %bitcast.5, f32[32,1,256]{2,1,0:T(1,128)} %bitcast.6, bf16[1,1,32,4,8192]{4,3,2,1,0:T(4,128)(2,1)} %vis_hbm.1, ...), custom_call_target="tpu_custom_call" | custom-call | tf_op jit(solution)/shard_map/pallas_call | solution.py:495
  65.8 0.7 %shard_map.86 = (bf16[1,1,32,4,256]{4,3,2,1,0:T(4,128)(2,1)}, bf16[1,1,32,4,1024]{4,3,2,1,0:T(4,128)(2,1)}, f32[4,2,128]{2,1,0:T(2,128)}) custom-call(bf16[1,1,32,4,256]{4,3,2,1,0:T(4,128)(2,1)S(1)} %get-tuple-element.9.kv, bf16[1,1,32,4,1024]{4,3,2,1,0:T(4,128)(2,1)S(1)} %get-tuple-element.10.vg, f32[4,2,128]{2,1,0:T(2,128)S(1)} %get-tuple-element.11.bg), custom_call_target="tpu_custom_call" | custom-call | tf_op jit(solution)/shard_map/pallas_call | solution.py:517

commit v7 on v6

--- a/solution.py
+++ b/solution.py
@@ -32,7 +32,7 @@
     kv_out, vg_out, bg_out,
     counts, bias, gain, vis, w, cot_own, cot_in, hop, xs, xn, inv, proj, kv_own, masked, coef,
     s1, r1, acc, s2, r2, s3, r3, vg,
-    p_own, p_in, z_own, z_in, f_own, kv_hop,
+    p_own, p_in, z_own, zb_own, z_in, f_own, kv_hop,
     cot_s, cot_r, kv_s, kv_r, z_s, z_r, p_s, p_r, f_s, f_r, kv_hop_s, kv_hop_r,
     s1_s, s1_r, s2_s, s2_r, s3_s, s3_r, hop_s, hop_r, loc, deep,
 ):
@@ -291,14 +291,26 @@
             q = q + p_in[g, t]
     z_own[...] = q
 
-    def z_copy(other, at):
-        return remote(z_own, z_in.at[at], z_s.at[other], z_r.at[at], enc=other)
-
-    @pl.loop(0, n_enc - 1)
-    def _(i):
-        step = (i + 1) // 2
-        z_copy(lax.rem(me + n_enc // 2 + step * (1 - 2 * lax.rem(i, 2)), n_enc), me).start()
-
+    blocks = n_enc // 4
+    base, place = me // 4 * 4, lax.rem(me, 4)
+
+    def z_copy(src, other, at):
+        return remote(src, z_in.at[at], z_s.at[other], z_r.at[at], enc=other)
+
+    near_block = [base + lax.rem(place + d, 4) for d in (2, 1, 3)]
+    steps = sorted(range(1, blocks), key=lambda d: -min(d, blocks - d))
+    across = [lax.rem(me + 4 * d, n_enc) for d in steps]
+    for other in near_block:
+        z_copy(z_own, other, me).start()
+    z_in[me] = q
+    for other in near_block:
+        z_copy(z_own, other, other).wait_recv()
+    q = z_in[base]
+    for d in range(1, 4):
+        q = q + z_in[base + d]
+    zb_own[...] = q
+    for other in across:
+        z_copy(zb_own, other, me).start()
     z_in[me] = q
 
     @pl.loop(0, far)
@@ -365,14 +377,11 @@
     put_vg = pltpu.make_async_copy(vg, vg_out.at[0, 0], loc.at[7])
     put_vg.start()
 
-    @pl.loop(0, n_enc - 1)
-    def _(i):
-        other = lax.rem(me + 1 + i, n_enc)
-        z_copy(other, other).wait_recv()
-
-    q = z_in[0]
-    for s in range(1, n_enc):
-        q = q + z_in[s]
+    for other in across:
+        z_copy(zb_own, other, other).wait_recv()
+    q = z_in[place]
+    for d in range(1, blocks):
+        q = q + z_in[4 * d + place]
     f_own[...] = q
 
     def f_copy(other, at):
@@ -393,7 +402,6 @@
         kv_copy(other, other).wait_recv()
         kv_copy(other, me).wait_send()
         cot_copy(other, me).wait_send()
-        z_copy(other, me).wait_send()
 
     @pl.loop(0, far)
     def _(i):
@@ -409,6 +417,10 @@
     def _(i):
         p_copy(*in_plane(i), group, rank).wait_send()
 
+    for other in near_block:
+        z_copy(z_own, other, me).wait_send()
+    for other in across:
+        z_copy(zb_own, other, me).wait_send()
     for k in range(RING):
         s1_copy(k).wait_send()
     for side in range(2):
@@ -472,6 +484,7 @@
         vmem((n_enc, cap, own), bf16),
         vmem((n_llm, n_tp, q_rows, LANES), f32),
         vmem((n_llm, n_tp, q_rows, LANES), f32),
+        vmem((q_rows, LANES), f32),
         vmem((q_rows, LANES), f32),
         vmem((n_enc, q_rows, LANES), f32),
         vmem((q_rows, LANES), f32),

time: 66.7 us -> 67.4 us (1.010)
  no operation moved by 1% of the time
where the time goes in v7:
time: 67.4 us; the launch traced here: 66.9 us
  Pallas kernels  66.2 us (98%)
    pallas_call x1, Pallas kernels, per_device(): pl.pallas_call(kernel, out_shape=results, in_specs=[in_hbm] * 6, out_spec...  65.5 us

profile of v7, /device:TPU:1, one launch (start us, length us, event | category | flops | bytes accessed | tf_op | source)
XLA Modules:
  0.0 66.9 jit_solution(9952956208796294156)
XLA Ops:
  0.6 65.5 %shard_map.85 = (bf16[1,1,32,4,256]{4,3,2,1,0:T(4,128)(2,1)S(1)}, bf16[1,1,32,4,1024]{4,3,2,1,0:T(4,128)(2,1)S(1)}, f32[4,2,128]{2,1,0:T(2,128)S(1)}) custom-call(s32[1,1,32]{2,1,0:T(1,128)} %counts_hbm.1, f32[1,8192]{1,0:T(1,128)} %bitcast.5, f32[32,1,256]{2,1,0:T(1,128)} %bitcast.6, bf16[1,1,32,4,8192]{4,3,2,1,0:T(4,128)(2,1)} %vis_hbm.1, ...), custom_call_target="tpu_custom_call" | custom-call | tf_op jit(solution)/shard_map/pallas_call | solution.py:508
  66.1 0.7 %shard_map.86 = (bf16[1,1,32,4,256]{4,3,2,1,0:T(4,128)(2,1)}, bf16[1,1,32,4,1024]{4,3,2,1,0:T(4,128)(2,1)}, f32[4,2,128]{2,1,0:T(2,128)}) custom-call(bf16[1,1,32,4,256]{4,3,2,1,0:T(4,128)(2,1)S(1)} %get-tuple-element.9.kv, bf16[1,1,32,4,1024]{4,3,2,1,0:T(4,128)(2,1)S(1)} %get-tuple-element.10.vg, f32[4,2,128]{2,1,0:T(2,128)S(1)} %get-tuple-element.11.bg), custom_call_target="tpu_custom_call" | custom-call | tf_op jit(solution)/shard_map/pallas_call | solution.py:530
